TPU v7x, 32 devices: a whole 2x2x4 slice. The times are simulated.
32 devices in a mesh: seq: 8 (over z, core), tp: 4 (over y, x).
Axes of the slice: x: 2, y: 2, z: 4, core: 2. Of those that a mesh axis runs over, the one named last changes fastest.
Arguments:
- q_heads: bfloat16 [1024, 4096], P('seq', 'tp'), may hold values from -200 to 200
- k_heads: bfloat16 [1024, 4096], P('seq', 'tp'), may hold values from -4 to 4
- v_heads: bfloat16 [1024, 4096], P('seq', 'tp'), may hold values from -5 to 5
- grad_attn: bfloat16 [1024, 4096], P('seq', 'tp'), may hold values from -5 to 5
- attn_out: bfloat16 [1024, 4096], P('seq', 'tp'), may hold values from -5 to 5
- gate_q: bfloat16 [1024, 8192], P('seq', 'tp'), may hold values from -5 to 5
- feat_k: bfloat16 [1024, 8192], P('seq', 'tp'), may hold values from -5 to 5
- feat_v: bfloat16 [1024, 8192], P('seq', 'tp'), may hold values from -5 to 5
- conv_out: bfloat16 [1024, 8192], P('seq', 'tp'), may hold values from -5 to 5
- grad_y: bfloat16 [1024, 8192], P('seq', 'tp'), may hold values from -5 to 5
- filters: float32 [64, 128], replicated, may hold values from -0.5 to 0.5
Outputs:
- grad_q: bfloat16 [1024, 4096], P('seq', 'tp')
- grad_k: bfloat16 [1024, 4096], P('seq', 'tp')
- grad_v: bfloat16 [1024, 4096], P('seq', 'tp')
- grad_gate: bfloat16 [1024, 8192], P('seq', 'tp')
- grad_feat_k: bfloat16 [1024, 8192], P('seq', 'tp')
- grad_feat_v: bfloat16 [1024, 8192], P('seq', 'tp')
- grad_filters: float32 [64, 128], replicated
All inputs are finite; a program needn't handle non-finite values.
Results may differ from a plain program's by a relative error of at most 0.014.
Values may be sent and summed in bfloat16 or wider, within the bound.
A program may use at most 64 MiB of HBM per device.

v0:
```python
import jax
import jax.numpy as jnp
from jax import lax
from jax.sharding import PartitionSpec as P

HEADS = 32


def from_behind(value, axis, steps):
    count = lax.axis_size(axis)
    leading, last = (max(0, -steps), min(count, count - steps))
    return lax.ppermute(value, axis, [(source, source + steps) for source in range(leading, last)])


def wire_parts(x):
    high = x.astype(jnp.bfloat16)
    back = lax.optimization_barrier(high).astype(jnp.float32)
    low = (x - back).astype(jnp.bfloat16)
    return (high, low)


def local(
    q_heads,
    k_heads,
    v_heads,
    grad_attn,
    attn_out,
    gate_q,
    feat_k,
    feat_v,
    conv_out,
    grad_y,
    filters,
):
    rows = q_heads.shape[0]
    heads_here = HEADS // lax.axis_size("tp")
    width = q_heads.shape[1] // heads_here
    scale = 1.0 / width**0.5
    shards = lax.axis_size("seq")
    place = lax.axis_index("seq")
    queries = q_heads.reshape(rows, heads_here, width)
    upstream = grad_attn.reshape(rows, heads_here, width)
    keys_here = k_heads.reshape(rows, heads_here, width)
    values_here = v_heads.reshape(rows, heads_here, width)
    delta = jnp.sum(
        upstream.astype(jnp.float32)
        * attn_out.reshape(rows, heads_here, width).astype(jnp.float32),
        axis=2,
    )
    delta_heads = delta.T
    diagonal = jnp.arange(rows)[:, None] >= jnp.arange(rows)[None, :]

    def query_tile(state, key_piece, value_piece, live):
        top, total, acc = state
        count = key_piece.shape[0]
        key_block = key_piece.reshape(count, heads_here, width)
        value_block = value_piece.reshape(count, heads_here, width)
        scores = (
            jnp.einsum("qhd,khd->hqk", queries, key_block, preferred_element_type=jnp.float32)
            * scale
        )
        top_new = jnp.maximum(top, jnp.max(jnp.where(live[None], scores, -1e30), axis=2))
        weights = jnp.where(live[None], jnp.exp(scores - top_new[:, :, None]), 0.0)
        decay = jnp.exp(top - top_new)
        dprob = jnp.einsum(
            "qhd,khd->hqk", upstream, value_block, preferred_element_type=jnp.float32
        )
        term = jnp.einsum(
            "hqk,khd->qhd",
            weights * (dprob - delta_heads[:, :, None]),
            key_block.astype(jnp.float32),
            precision=lax.Precision.HIGHEST,
        )
        return (top_new, total * decay + jnp.sum(weights, axis=2), acc * decay.T[:, :, None] + term)

    zero_rows = jnp.zeros((rows, heads_here, width), jnp.float32)
    state = (
        jnp.full((heads_here, rows), -1e30, jnp.float32),
        jnp.zeros((heads_here, rows), jnp.float32),
        zero_rows,
    )
    state = query_tile(state, k_heads, v_heads, diagonal)

    def relay_keys(back, carry):
        inner, moving = carry
        moving = from_behind((moving[0], moving[1]), "seq", 1)
        valid = place >= back
        live = jnp.broadcast_to(valid, (rows, rows))
        inner = query_tile(inner, moving[0], moving[1], live)
        return (inner, moving)

    state, moved = lax.fori_loop(1, shards, relay_keys, (state, (k_heads, v_heads)))
    top, total, acc = state
    lse = (top + jnp.log(total)).T
    grad_query = acc * (1.0 / total).T[:, :, None] * scale
    lse_high, lse_low = wire_parts(lse)
    delta_high, delta_low = wire_parts(delta)
    stats = jnp.stack([lse_high, lse_low, delta_high, delta_low], axis=1)

    def key_tile(inner, query_piece, upstream_piece, stat_piece, live):
        key_grad, value_grad = inner
        count = query_piece.shape[0]
        query_block = query_piece.reshape(count, heads_here, width)
        upstream_block = upstream_piece.reshape(count, heads_here, width)
        lse_w = stat_piece[:, 0].astype(jnp.float32) + stat_piece[:, 1].astype(jnp.float32)
        delta_w = stat_piece[:, 2].astype(jnp.float32) + stat_piece[:, 3].astype(jnp.float32)
        scores = (
            jnp.einsum("qhd,khd->hqk", query_block, keys_here, preferred_element_type=jnp.float32)
            * scale
        )
        probs = jnp.where(live[None], jnp.exp(scores - lse_w.T[:, :, None]), 0.0)
        dprob = jnp.einsum(
            "qhd,khd->hqk", upstream_block, values_here, preferred_element_type=jnp.float32
        )
        dscore = probs * (dprob - delta_w.T[:, :, None])
        value_grad = value_grad + jnp.einsum(
            "hqk,qhd->khd",
            probs.astype(jnp.bfloat16),
            upstream_block,
            preferred_element_type=jnp.float32,
        )
        key_grad = key_grad + jnp.einsum(
            "hqk,qhd->khd",
            dscore.astype(jnp.bfloat16),
            query_block,
            preferred_element_type=jnp.float32,
        )
        return (key_grad, value_grad)

    grads = (zero_rows, zero_rows)
    grads = key_tile(grads, q_heads, grad_attn, stats, diagonal)

    def relay_queries(back, carry):
        inner, moving = carry
        moving = from_behind((moving[0], moving[1], moving[2]), "seq", -1)
        valid = place + back <= shards - 1
        live = jnp.broadcast_to(valid, (rows, rows))
        inner = key_tile(inner, moving[0], moving[1], moving[2], live)
        return (inner, moving)

    grads, moved = lax.fori_loop(1, shards, relay_queries, (grads, (q_heads, grad_attn, stats)))
    key_grad, value_grad = grads
    grad_q = grad_query.astype(jnp.bfloat16).reshape(rows, heads_here * width)
    grad_k = (key_grad * scale).astype(jnp.bfloat16).reshape(rows, heads_here * width)
    grad_v = value_grad.astype(jnp.bfloat16).reshape(rows, heads_here * width)
    span_taps = filters.shape[1]
    groups = filters.shape[0]
    channels = gate_q.shape[1]
    dz = (grad_y.astype(jnp.float32) * gate_q.astype(jnp.float32)).astype(jnp.bfloat16)
    rim = from_behind(dz[: span_taps - 1], "seq", -1)
    grad_gate = (grad_y.astype(jnp.float32) * conv_out.astype(jnp.float32)).astype(jnp.bfloat16)
    padded = jnp.concatenate([dz, rim], axis=0).astype(jnp.float32)
    taps = jnp.tile(filters.T, (1, channels // groups))
    mixed = feat_k.astype(jnp.float32) * feat_v.astype(jnp.float32)
    numbers = ("NWC", "WIO", "NWC")
    dw = lax.conv_general_dilated(
        padded[None],
        taps[:, None, :],
        (1,),
        "VALID",
        dimension_numbers=numbers,
        feature_group_count=channels,
        precision=lax.Precision.HIGHEST,
    )[0]
    local_terms = lax.conv_general_dilated(
        padded[None],
        mixed[:, None, :],
        (1,),
        "VALID",
        dimension_numbers=numbers,
        feature_group_count=channels,
        precision=lax.Precision.HIGHEST,
    )[0]
    grad_feat_k = (dw * feat_v.astype(jnp.float32)).astype(jnp.bfloat16)
    grad_feat_v = (dw * feat_k.astype(jnp.float32)).astype(jnp.bfloat16)
    local_terms = jnp.sum(local_terms.reshape(span_taps, channels // groups, groups), axis=1).T
    filter_total = lax.psum(local_terms, ("seq", "tp"))
    count_all = rows * shards * channels * lax.axis_size("tp") / groups
    grad_filters = filter_total * (1.0 / count_all**0.5)
    return (grad_q, grad_k, grad_v, grad_gate, grad_feat_k, grad_feat_v, grad_filters)


def solution(mesh):
    in_specs = (
        P("seq", "tp"),
        P("seq", "tp"),
        P("seq", "tp"),
        P("seq", "tp"),
        P("seq", "tp"),
        P("seq", "tp"),
        P("seq", "tp"),
        P("seq", "tp"),
        P("seq", "tp"),
        P("seq", "tp"),
        P(),
    )
    out_specs = (
        P("seq", "tp"),
        P("seq", "tp"),
        P("seq", "tp"),
        P("seq", "tp"),
        P("seq", "tp"),
        P("seq", "tp"),
        P(),
    )
    return jax.shard_map(local, mesh=mesh, in_specs=in_specs, out_specs=out_specs, check_vma=False)
```

profile of v0, /device:TPU:0, one launch (start us, length us, event | category | flops | bytes accessed | tf_op | source)
XLA Modules:
  0.0 252.8 jit_solution(9573498819342594499)
XLA Ops:
  8.7 79.7 %while.42 = (s32[]{:T(128)}, f32[8,128]{1,0:T(8,128)S(1)}, f32[8,128]{1,0:T(8,128)S(1)}, f32[128,8,128]{2,0,1:T(8,128)S(1)}, bf16[128,1024]{0,1:T(8,128)(2,1)S(1...) while((s32[]{:T(128)}, f32[8,128]{1,0:T(8,128)S(1)}, ...), condition=%wide.region_6.7_spmd, body=%wide.region_3.6_spmd.sunk | while | flops 270011392 | bytes 8196297 | solution.py:92
  11.7 4.6 %collective-permute-start.1 = (bf16[128,1024]{0,1:T(8,128)(2,1)S(1)}, bf16[128,1024]{0,1:T(8,128)(2,1)S(1)}, u32[]{:S(2)}, u32[]{:S(2)}) collective-permute-start(bf16[128,1024]{0,1:T(8,128)(2,1)S(1)} %get-tuple-element.619), channel_id=1, source_target_pairs={{0,4},{4,8},{8,12},{12,16},{16,20},{20,24},{24,28},{1,5},{5,9},{9,... | collective-permute-start | bytes 786440 | tf_op jit(solution)/shard_map/while/body/eval_jaxpr/ppermute | solution.py:12
  18.6 5.0 %collective-permute-start = (bf16[128,1024]{0,1:T(8,128)(2,1)S(1)}, bf16[128,1024]{0,1:T(8,128)(2,1)S(1)}, u32[]{:S(2)}, u32[]{:S(2)}) collective-permute-start(bf16[128,1024]{0,1:T(8,128)(2,1)S(1)} %get-tuple-element.618), channel_id=1, source_target_pairs={{0,4},{4,8},{8,12},{12,16},{16,20},{20,24},{24,28},{1,5},{5,9},{9,... | collective-permute-start | bytes 786440 | tf_op jit(solution)/shard_map/while/body/eval_jaxpr/ppermute | solution.py:12
  23.5 4.4 %collective-permute-start.1 = (bf16[128,1024]{0,1:T(8,128)(2,1)S(1)}, bf16[128,1024]{0,1:T(8,128)(2,1)S(1)}, u32[]{:S(2)}, u32[]{:S(2)}) collective-permute-start(bf16[128,1024]{0,1:T(8,128)(2,1)S(1)} %get-tuple-element.619), channel_id=1, source_target_pairs={{0,4},{4,8},{8,12},{12,16},{16,20},{20,24},{24,28},{1,5},{5,9},{9,... | collective-permute-start | bytes 786440 | tf_op jit(solution)/shard_map/while/body/eval_jaxpr/ppermute | solution.py:12
  30.2 5.0 %collective-permute-start = (bf16[128,1024]{0,1:T(8,128)(2,1)S(1)}, bf16[128,1024]{0,1:T(8,128)(2,1)S(1)}, u32[]{:S(2)}, u32[]{:S(2)}) collective-permute-start(bf16[128,1024]{0,1:T(8,128)(2,1)S(1)} %get-tuple-element.618), channel_id=1, source_target_pairs={{0,4},{4,8},{8,12},{12,16},{16,20},{20,24},{24,28},{1,5},{5,9},{9,... | collective-permute-start | bytes 786440 | tf_op jit(solution)/shard_map/while/body/eval_jaxpr/ppermute | solution.py:12
  35.2 4.4 %collective-permute-start.1 = (bf16[128,1024]{0,1:T(8,128)(2,1)S(1)}, bf16[128,1024]{0,1:T(8,128)(2,1)S(1)}, u32[]{:S(2)}, u32[]{:S(2)}) collective-permute-start(bf16[128,1024]{0,1:T(8,128)(2,1)S(1)} %get-tuple-element.619), channel_id=1, source_target_pairs={{0,4},{4,8},{8,12},{12,16},{16,20},{20,24},{24,28},{1,5},{5,9},{9,... | collective-permute-start | bytes 786440 | tf_op jit(solution)/shard_map/while/body/eval_jaxpr/ppermute | solution.py:12
  41.8 5.0 %collective-permute-start = (bf16[128,1024]{0,1:T(8,128)(2,1)S(1)}, bf16[128,1024]{0,1:T(8,128)(2,1)S(1)}, u32[]{:S(2)}, u32[]{:S(2)}) collective-permute-start(bf16[128,1024]{0,1:T(8,128)(2,1)S(1)} %get-tuple-element.618), channel_id=1, source_target_pairs={{0,4},{4,8},{8,12},{12,16},{16,20},{20,24},{24,28},{1,5},{5,9},{9,... | collective-permute-start | bytes 786440 | tf_op jit(solution)/shard_map/while/body/eval_jaxpr/ppermute | solution.py:12
  46.8 4.4 %collective-permute-start.1 = (bf16[128,1024]{0,1:T(8,128)(2,1)S(1)}, bf16[128,1024]{0,1:T(8,128)(2,1)S(1)}, u32[]{:S(2)}, u32[]{:S(2)}) collective-permute-start(bf16[128,1024]{0,1:T(8,128)(2,1)S(1)} %get-tuple-element.619), channel_id=1, source_target_pairs={{0,4},{4,8},{8,12},{12,16},{16,20},{20,24},{24,28},{1,5},{5,9},{9,... | collective-permute-start | bytes 786440 | tf_op jit(solution)/shard_map/while/body/eval_jaxpr/ppermute | solution.py:12
  53.5 5.0 %collective-permute-start = (bf16[128,1024]{0,1:T(8,128)(2,1)S(1)}, bf16[128,1024]{0,1:T(8,128)(2,1)S(1)}, u32[]{:S(2)}, u32[]{:S(2)}) collective-permute-start(bf16[128,1024]{0,1:T(8,128)(2,1)S(1)} %get-tuple-element.618), channel_id=1, source_target_pairs={{0,4},{4,8},{8,12},{12,16},{16,20},{20,24},{24,28},{1,5},{5,9},{9,... | collective-permute-start | bytes 786440 | tf_op jit(solution)/shard_map/while/body/eval_jaxpr/ppermute | solution.py:12
  58.4 4.4 %collective-permute-start.1 = (bf16[128,1024]{0,1:T(8,128)(2,1)S(1)}, bf16[128,1024]{0,1:T(8,128)(2,1)S(1)}, u32[]{:S(2)}, u32[]{:S(2)}) collective-permute-start(bf16[128,1024]{0,1:T(8,128)(2,1)S(1)} %get-tuple-element.619), channel_id=1, source_target_pairs={{0,4},{4,8},{8,12},{12,16},{16,20},{20,24},{24,28},{1,5},{5,9},{9,... | collective-permute-start | bytes 786440 | tf_op jit(solution)/shard_map/while/body/eval_jaxpr/ppermute | solution.py:12
  65.1 5.0 %collective-permute-start = (bf16[128,1024]{0,1:T(8,128)(2,1)S(1)}, bf16[128,1024]{0,1:T(8,128)(2,1)S(1)}, u32[]{:S(2)}, u32[]{:S(2)}) collective-permute-start(bf16[128,1024]{0,1:T(8,128)(2,1)S(1)} %get-tuple-element.618), channel_id=1, source_target_pairs={{0,4},{4,8},{8,12},{12,16},{16,20},{20,24},{24,28},{1,5},{5,9},{9,... | collective-permute-start | bytes 786440 | tf_op jit(solution)/shard_map/while/body/eval_jaxpr/ppermute | solution.py:12
  70.1 4.4 %collective-permute-start.1 = (bf16[128,1024]{0,1:T(8,128)(2,1)S(1)}, bf16[128,1024]{0,1:T(8,128)(2,1)S(1)}, u32[]{:S(2)}, u32[]{:S(2)}) collective-permute-start(bf16[128,1024]{0,1:T(8,128)(2,1)S(1)} %get-tuple-element.619), channel_id=1, source_target_pairs={{0,4},{4,8},{8,12},{12,16},{16,20},{20,24},{24,28},{1,5},{5,9},{9,... | collective-permute-start | bytes 786440 | tf_op jit(solution)/shard_map/while/body/eval_jaxpr/ppermute | solution.py:12
  76.7 5.0 %collective-permute-start = (bf16[128,1024]{0,1:T(8,128)(2,1)S(1)}, bf16[128,1024]{0,1:T(8,128)(2,1)S(1)}, u32[]{:S(2)}, u32[]{:S(2)}) collective-permute-start(bf16[128,1024]{0,1:T(8,128)(2,1)S(1)} %get-tuple-element.618), channel_id=1, source_target_pairs={{0,4},{4,8},{8,12},{12,16},{16,20},{20,24},{24,28},{1,5},{5,9},{9,... | collective-permute-start | bytes 786440 | tf_op jit(solution)/shard_map/while/body/eval_jaxpr/ppermute | solution.py:12
  81.7 4.4 %collective-permute-start.1 = (bf16[128,1024]{0,1:T(8,128)(2,1)S(1)}, bf16[128,1024]{0,1:T(8,128)(2,1)S(1)}, u32[]{:S(2)}, u32[]{:S(2)}) collective-permute-start(bf16[128,1024]{0,1:T(8,128)(2,1)S(1)} %get-tuple-element.619), channel_id=1, source_target_pairs={{0,4},{4,8},{8,12},{12,16},{16,20},{20,24},{24,28},{1,5},{5,9},{9,... | collective-permute-start | bytes 786440 | tf_op jit(solution)/shard_map/while/body/eval_jaxpr/ppermute | solution.py:12
  89.8 87.0 %while.43 = (s32[]{:T(128)}, f32[128,8,128]{2,0,1:T(8,128)S(1)}, f32[128,8,128]{2,0,1:T(8,128)S(1)}, bf16[128,1024]{0,1:T(8,128)(2,1)S(1)}, bf16[128,1024]{0,1:T...) while((s32[]{:T(128)}, f32[128,8,128]{2,0,1:T(8,128)S(1)}, ...), condition=%wide.region_8.9_spmd, body=%wide.region_7.8_spmd.sunk | while | flops 135403520 | bytes 8462587 | solution.py:141
  104.5 6.1 %collective-permute-done.3 = bf16[128,4,8]{0,2,1:T(8,128)(2,1)S(1)} collective-permute-done((bf16[128,4,8]{0,2,1:T(8,128)(2,1)S(1)}, bf16[128,4,8]{0,2,1:T(8,128)(2,1)S(1)}, u32[]{:S(2)}, u32[]{:S(2)}) %collective-permute-start.3) | collective-permute-done | bytes 8224 | tf_op jit(solution)/shard_map/while/body/eval_jaxpr/ppermute | solution.py:12
  117.8 5.4 %collective-permute-done.3 = bf16[128,4,8]{0,2,1:T(8,128)(2,1)S(1)} collective-permute-done((bf16[128,4,8]{0,2,1:T(8,128)(2,1)S(1)}, bf16[128,4,8]{0,2,1:T(8,128)(2,1)S(1)}, u32[]{:S(2)}, u32[]{:S(2)}) %collective-permute-start.3) | collective-permute-done | bytes 8224 | tf_op jit(solution)/shard_map/while/body/eval_jaxpr/ppermute | solution.py:12
  130.4 5.4 %collective-permute-done.3 = bf16[128,4,8]{0,2,1:T(8,128)(2,1)S(1)} collective-permute-done((bf16[128,4,8]{0,2,1:T(8,128)(2,1)S(1)}, bf16[128,4,8]{0,2,1:T(8,128)(2,1)S(1)}, u32[]{:S(2)}, u32[]{:S(2)}) %collective-permute-start.3) | collective-permute-done | bytes 8224 | tf_op jit(solution)/shard_map/while/body/eval_jaxpr/ppermute | solution.py:12
  143.0 5.3 %collective-permute-done.3 = bf16[128,4,8]{0,2,1:T(8,128)(2,1)S(1)} collective-permute-done((bf16[128,4,8]{0,2,1:T(8,128)(2,1)S(1)}, bf16[128,4,8]{0,2,1:T(8,128)(2,1)S(1)}, u32[]{:S(2)}, u32[]{:S(2)}) %collective-permute-start.3) | collective-permute-done | bytes 8224 | tf_op jit(solution)/shard_map/while/body/eval_jaxpr/ppermute | solution.py:12
  155.5 5.3 %collective-permute-done.3 = bf16[128,4,8]{0,2,1:T(8,128)(2,1)S(1)} collective-permute-done((bf16[128,4,8]{0,2,1:T(8,128)(2,1)S(1)}, bf16[128,4,8]{0,2,1:T(8,128)(2,1)S(1)}, u32[]{:S(2)}, u32[]{:S(2)}) %collective-permute-start.3) | collective-permute-done | bytes 8224 | tf_op jit(solution)/shard_map/while/body/eval_jaxpr/ppermute | solution.py:12
  168.1 5.3 %collective-permute-done.3 = bf16[128,4,8]{0,2,1:T(8,128)(2,1)S(1)} collective-permute-done((bf16[128,4,8]{0,2,1:T(8,128)(2,1)S(1)}, bf16[128,4,8]{0,2,1:T(8,128)(2,1)S(1)}, u32[]{:S(2)}, u32[]{:S(2)}) %collective-permute-start.3) | collective-permute-done | bytes 8224 | tf_op jit(solution)/shard_map/while/body/eval_jaxpr/ppermute | solution.py:12
  181.6 11.6 %fusion.15 = f32[1,128,2048]{2,0,1:T(1,128)S(1)} fusion(f32[128,1,2048]{2,1,0:T(1,128)S(1)} %copy.197, bf16[1,255,2048]{2,1,0:T(8,128)(2,1)S(1)} %maximum_bitcast_fusion), kind=kOutput, calls=%fused_computation.28 | convolution fusion | flops 402653184 | bytes 3141632 | tf_op jit(solution)/shard_map/conv_general_dilated | solution.py:156
  194.7 11.7 %fusion.13 = f32[1,128,2048]{2,0,1:T(1,128)S(1)} fusion(bf16[1,255,2048]{2,1,0:T(8,128)(2,1)S(1)} %maximum_bitcast_fusion, f32[128,1,2048]{2,0,1:T(8,128)S(1)} %get-tuple-element.462), kind=kOutput, calls=%fused_computation.26 | convolution fusion | flops 402653184 | bytes 3141632 | tf_op jit(solution)/shard_map/conv_general_dilated | solution.py:165
  207.2 44.9 %psum.7 = f32[64,128]{1,0:T(8,128)S(1)} all-reduce(f32[64,128]{1,0:T(8,128)S(1)} %bitcast.177), channel_id=1, replica_groups=mesh['seq'=8,'tp'=4] {'seq','tp'}, use_global_device_ids=true, to_apply=%region_10.11 | all-reduce | flops 8192 | bytes 65536 | tf_op jit(solution)/shard_map/psum | solution.py:177
  (230 shorter events, 88.8 us)
Async XLA Ops:
  3.4 176.9 %collective-permute-start.5 = (bf16[127,2048]{1,0:T(8,128)(2,1)}, bf16[127,2048]{1,0:T(8,128)(2,1)}, u32[]{:S(2)}, u32[]{:S(2)}) collective-permute-start(bf16[127,2048]{1,0:T(8,128)(2,1)} %bitcast.110), channel_id=1, source_target_pairs={{4,0},{8,4},{12,8},{16,12},{20,16},{24,20},{28,24},{5,1},{9,5},{13... | collective-permute-start | bytes 1560584 | tf_op jit(solution)/shard_map/ppermute | solution.py:12
  18.6 9.4 %collective-permute-start = (bf16[128,1024]{0,1:T(8,128)(2,1)S(1)}, bf16[128,1024]{0,1:T(8,128)(2,1)S(1)}, u32[]{:S(2)}, u32[]{:S(2)}) collective-permute-start(bf16[128,1024]{0,1:T(8,128)(2,1)S(1)} %get-tuple-element.618), channel_id=1, source_target_pairs={{0,4},{4,8},{8,12},{12,16},{16,20},{20,24},{24,28},{1,5},{5,9},{9,... | collective-permute-start | bytes 786440 | tf_op jit(solution)/shard_map/while/body/eval_jaxpr/ppermute | solution.py:12
  30.2 9.4 %collective-permute-start = (bf16[128,1024]{0,1:T(8,128)(2,1)S(1)}, bf16[128,1024]{0,1:T(8,128)(2,1)S(1)}, u32[]{:S(2)}, u32[]{:S(2)}) collective-permute-start(bf16[128,1024]{0,1:T(8,128)(2,1)S(1)} %get-tuple-element.618), channel_id=1, source_target_pairs={{0,4},{4,8},{8,12},{12,16},{16,20},{20,24},{24,28},{1,5},{5,9},{9,... | collective-permute-start | bytes 786440 | tf_op jit(solution)/shard_map/while/body/eval_jaxpr/ppermute | solution.py:12
  41.8 9.4 %collective-permute-start = (bf16[128,1024]{0,1:T(8,128)(2,1)S(1)}, bf16[128,1024]{0,1:T(8,128)(2,1)S(1)}, u32[]{:S(2)}, u32[]{:S(2)}) collective-permute-start(bf16[128,1024]{0,1:T(8,128)(2,1)S(1)} %get-tuple-element.618), channel_id=1, source_target_pairs={{0,4},{4,8},{8,12},{12,16},{16,20},{20,24},{24,28},{1,5},{5,9},{9,... | collective-permute-start | bytes 786440 | tf_op jit(solution)/shard_map/while/body/eval_jaxpr/ppermute | solution.py:12
  53.5 9.4 %collective-permute-start = (bf16[128,1024]{0,1:T(8,128)(2,1)S(1)}, bf16[128,1024]{0,1:T(8,128)(2,1)S(1)}, u32[]{:S(2)}, u32[]{:S(2)}) collective-permute-start(bf16[128,1024]{0,1:T(8,128)(2,1)S(1)} %get-tuple-element.618), channel_id=1, source_target_pairs={{0,4},{4,8},{8,12},{12,16},{16,20},{20,24},{24,28},{1,5},{5,9},{9,... | collective-permute-start | bytes 786440 | tf_op jit(solution)/shard_map/while/body/eval_jaxpr/ppermute | solution.py:12
  65.1 9.4 %collective-permute-start = (bf16[128,1024]{0,1:T(8,128)(2,1)S(1)}, bf16[128,1024]{0,1:T(8,128)(2,1)S(1)}, u32[]{:S(2)}, u32[]{:S(2)}) collective-permute-start(bf16[128,1024]{0,1:T(8,128)(2,1)S(1)} %get-tuple-element.618), channel_id=1, source_target_pairs={{0,4},{4,8},{8,12},{12,16},{16,20},{20,24},{24,28},{1,5},{5,9},{9,... | collective-permute-start | bytes 786440 | tf_op jit(solution)/shard_map/while/body/eval_jaxpr/ppermute | solution.py:12
  76.7 9.4 %collective-permute-start = (bf16[128,1024]{0,1:T(8,128)(2,1)S(1)}, bf16[128,1024]{0,1:T(8,128)(2,1)S(1)}, u32[]{:S(2)}, u32[]{:S(2)}) collective-permute-start(bf16[128,1024]{0,1:T(8,128)(2,1)S(1)} %get-tuple-element.618), channel_id=1, source_target_pairs={{0,4},{4,8},{8,12},{12,16},{16,20},{20,24},{24,28},{1,5},{5,9},{9,... | collective-permute-start | bytes 786440 | tf_op jit(solution)/shard_map/while/body/eval_jaxpr/ppermute | solution.py:12
  100.6 10.0 %collective-permute-start.2 = (bf16[128,1024]{0,1:T(8,128)(2,1)S(1)}, bf16[128,1024]{0,1:T(8,128)(2,1)S(1)}, u32[]{:S(2)}, u32[]{:S(2)}) collective-permute-start(bf16[128,1024]{0,1:T(8,128)(2,1)S(1)} %get-tuple-element.650), channel_id=1, source_target_pairs={{4,0},{8,4},{12,8},{16,12},{20,16},{24,20},{28,24},{5,1},{9,5},{13... | collective-permute-start | bytes 786440 | tf_op jit(solution)/shard_map/while/body/eval_jaxpr/ppermute | solution.py:12
  101.9 8.7 %collective-permute-start.3 = (bf16[128,4,8]{0,2,1:T(8,128)(2,1)S(1)}, bf16[128,4,8]{0,2,1:T(8,128)(2,1)S(1)}, u32[]{:S(2)}, u32[]{:S(2)}) collective-permute-start(bf16[128,4,8]{0,2,1:T(8,128)(2,1)S(1)} %get-tuple-element.652), channel_id=1, source_target_pairs={{4,0},{8,4},{12,8},{16,12},{20,16},{24,20},{28,24},{5,1},{9,5},{13... | collective-permute-start | bytes 24584 | tf_op jit(solution)/shard_map/while/body/eval_jaxpr/ppermute | solution.py:12
  103.2 9.7 %collective-permute-start.4 = (bf16[128,1024]{0,1:T(8,128)(2,1)S(1)}, bf16[128,1024]{0,1:T(8,128)(2,1)S(1)}, u32[]{:S(2)}, u32[]{:S(2)}) collective-permute-start(bf16[128,1024]{0,1:T(8,128)(2,1)S(1)} %get-tuple-element.651), channel_id=1, source_target_pairs={{4,0},{8,4},{12,8},{16,12},{20,16},{24,20},{28,24},{5,1},{9,5},{13... | collective-permute-start | bytes 786440 | tf_op jit(solution)/shard_map/while/body/eval_jaxpr/ppermute | solution.py:12
  113.9 9.3 %collective-permute-start.2 = (bf16[128,1024]{0,1:T(8,128)(2,1)S(1)}, bf16[128,1024]{0,1:T(8,128)(2,1)S(1)}, u32[]{:S(2)}, u32[]{:S(2)}) collective-permute-start(bf16[128,1024]{0,1:T(8,128)(2,1)S(1)} %get-tuple-element.650), channel_id=1, source_target_pairs={{4,0},{8,4},{12,8},{16,12},{20,16},{24,20},{28,24},{5,1},{9,5},{13... | collective-permute-start | bytes 786440 | tf_op jit(solution)/shard_map/while/body/eval_jaxpr/ppermute | solution.py:12
  115.2 8.0 %collective-permute-start.3 = (bf16[128,4,8]{0,2,1:T(8,128)(2,1)S(1)}, bf16[128,4,8]{0,2,1:T(8,128)(2,1)S(1)}, u32[]{:S(2)}, u32[]{:S(2)}) collective-permute-start(bf16[128,4,8]{0,2,1:T(8,128)(2,1)S(1)} %get-tuple-element.652), channel_id=1, source_target_pairs={{4,0},{8,4},{12,8},{16,12},{20,16},{24,20},{28,24},{5,1},{9,5},{13... | collective-permute-start | bytes 24584 | tf_op jit(solution)/shard_map/while/body/eval_jaxpr/ppermute | solution.py:12
  116.5 9.0 %collective-permute-start.4 = (bf16[128,1024]{0,1:T(8,128)(2,1)S(1)}, bf16[128,1024]{0,1:T(8,128)(2,1)S(1)}, u32[]{:S(2)}, u32[]{:S(2)}) collective-permute-start(bf16[128,1024]{0,1:T(8,128)(2,1)S(1)} %get-tuple-element.651), channel_id=1, source_target_pairs={{4,0},{8,4},{12,8},{16,12},{20,16},{24,20},{28,24},{5,1},{9,5},{13... | collective-permute-start | bytes 786440 | tf_op jit(solution)/shard_map/while/body/eval_jaxpr/ppermute | solution.py:12
  126.5 9.3 %collective-permute-start.2 = (bf16[128,1024]{0,1:T(8,128)(2,1)S(1)}, bf16[128,1024]{0,1:T(8,128)(2,1)S(1)}, u32[]{:S(2)}, u32[]{:S(2)}) collective-permute-start(bf16[128,1024]{0,1:T(8,128)(2,1)S(1)} %get-tuple-element.650), channel_id=1, source_target_pairs={{4,0},{8,4},{12,8},{16,12},{20,16},{24,20},{28,24},{5,1},{9,5},{13... | collective-permute-start | bytes 786440 | tf_op jit(solution)/shard_map/while/body/eval_jaxpr/ppermute | solution.py:12
  127.8 8.0 %collective-permute-start.3 = (bf16[128,4,8]{0,2,1:T(8,128)(2,1)S(1)}, bf16[128,4,8]{0,2,1:T(8,128)(2,1)S(1)}, u32[]{:S(2)}, u32[]{:S(2)}) collective-permute-start(bf16[128,4,8]{0,2,1:T(8,128)(2,1)S(1)} %get-tuple-element.652), channel_id=1, source_target_pairs={{4,0},{8,4},{12,8},{16,12},{20,16},{24,20},{28,24},{5,1},{9,5},{13... | collective-permute-start | bytes 24584 | tf_op jit(solution)/shard_map/while/body/eval_jaxpr/ppermute | solution.py:12
  129.1 9.0 %collective-permute-start.4 = (bf16[128,1024]{0,1:T(8,128)(2,1)S(1)}, bf16[128,1024]{0,1:T(8,128)(2,1)S(1)}, u32[]{:S(2)}, u32[]{:S(2)}) collective-permute-start(bf16[128,1024]{0,1:T(8,128)(2,1)S(1)} %get-tuple-element.651), channel_id=1, source_target_pairs={{4,0},{8,4},{12,8},{16,12},{20,16},{24,20},{28,24},{5,1},{9,5},{13... | collective-permute-start | bytes 786440 | tf_op jit(solution)/shard_map/while/body/eval_jaxpr/ppermute | solution.py:12
  139.1 9.3 %collective-permute-start.2 = (bf16[128,1024]{0,1:T(8,128)(2,1)S(1)}, bf16[128,1024]{0,1:T(8,128)(2,1)S(1)}, u32[]{:S(2)}, u32[]{:S(2)}) collective-permute-start(bf16[128,1024]{0,1:T(8,128)(2,1)S(1)} %get-tuple-element.650), channel_id=1, source_target_pairs={{4,0},{8,4},{12,8},{16,12},{20,16},{24,20},{28,24},{5,1},{9,5},{13... | collective-permute-start | bytes 786440 | tf_op jit(solution)/shard_map/while/body/eval_jaxpr/ppermute | solution.py:12
  140.4 8.0 %collective-permute-start.3 = (bf16[128,4,8]{0,2,1:T(8,128)(2,1)S(1)}, bf16[128,4,8]{0,2,1:T(8,128)(2,1)S(1)}, u32[]{:S(2)}, u32[]{:S(2)}) collective-permute-start(bf16[128,4,8]{0,2,1:T(8,128)(2,1)S(1)} %get-tuple-element.652), channel_id=1, source_target_pairs={{4,0},{8,4},{12,8},{16,12},{20,16},{24,20},{28,24},{5,1},{9,5},{13... | collective-permute-start | bytes 24584 | tf_op jit(solution)/shard_map/while/body/eval_jaxpr/ppermute | solution.py:12
  141.7 8.9 %collective-permute-start.4 = (bf16[128,1024]{0,1:T(8,128)(2,1)S(1)}, bf16[128,1024]{0,1:T(8,128)(2,1)S(1)}, u32[]{:S(2)}, u32[]{:S(2)}) collective-permute-start(bf16[128,1024]{0,1:T(8,128)(2,1)S(1)} %get-tuple-element.651), channel_id=1, source_target_pairs={{4,0},{8,4},{12,8},{16,12},{20,16},{24,20},{28,24},{5,1},{9,5},{13... | collective-permute-start | bytes 786440 | tf_op jit(solution)/shard_map/while/body/eval_jaxpr/ppermute | solution.py:12
  151.6 9.3 %collective-permute-start.2 = (bf16[128,1024]{0,1:T(8,128)(2,1)S(1)}, bf16[128,1024]{0,1:T(8,128)(2,1)S(1)}, u32[]{:S(2)}, u32[]{:S(2)}) collective-permute-start(bf16[128,1024]{0,1:T(8,128)(2,1)S(1)} %get-tuple-element.650), channel_id=1, source_target_pairs={{4,0},{8,4},{12,8},{16,12},{20,16},{24,20},{28,24},{5,1},{9,5},{13... | collective-permute-start | bytes 786440 | tf_op jit(solution)/shard_map/while/body/eval_jaxpr/ppermute | solution.py:12
  152.9 8.0 %collective-permute-start.3 = (bf16[128,4,8]{0,2,1:T(8,128)(2,1)S(1)}, bf16[128,4,8]{0,2,1:T(8,128)(2,1)S(1)}, u32[]{:S(2)}, u32[]{:S(2)}) collective-permute-start(bf16[128,4,8]{0,2,1:T(8,128)(2,1)S(1)} %get-tuple-element.652), channel_id=1, source_target_pairs={{4,0},{8,4},{12,8},{16,12},{20,16},{24,20},{28,24},{5,1},{9,5},{13... | collective-permute-start | bytes 24584 | tf_op jit(solution)/shard_map/while/body/eval_jaxpr/ppermute | solution.py:12
  154.2 8.9 %collective-permute-start.4 = (bf16[128,1024]{0,1:T(8,128)(2,1)S(1)}, bf16[128,1024]{0,1:T(8,128)(2,1)S(1)}, u32[]{:S(2)}, u32[]{:S(2)}) collective-permute-start(bf16[128,1024]{0,1:T(8,128)(2,1)S(1)} %get-tuple-element.651), channel_id=1, source_target_pairs={{4,0},{8,4},{12,8},{16,12},{20,16},{24,20},{28,24},{5,1},{9,5},{13... | collective-permute-start | bytes 786440 | tf_op jit(solution)/shard_map/while/body/eval_jaxpr/ppermute | solution.py:12
  164.2 9.3 %collective-permute-start.2 = (bf16[128,1024]{0,1:T(8,128)(2,1)S(1)}, bf16[128,1024]{0,1:T(8,128)(2,1)S(1)}, u32[]{:S(2)}, u32[]{:S(2)}) collective-permute-start(bf16[128,1024]{0,1:T(8,128)(2,1)S(1)} %get-tuple-element.650), channel_id=1, source_target_pairs={{4,0},{8,4},{12,8},{16,12},{20,16},{24,20},{28,24},{5,1},{9,5},{13... | collective-permute-start | bytes 786440 | tf_op jit(solution)/shard_map/while/body/eval_jaxpr/ppermute | solution.py:12
  166.8 8.9 %collective-permute-start.4 = (bf16[128,1024]{0,1:T(8,128)(2,1)S(1)}, bf16[128,1024]{0,1:T(8,128)(2,1)S(1)}, u32[]{:S(2)}, u32[]{:S(2)}) collective-permute-start(bf16[128,1024]{0,1:T(8,128)(2,1)S(1)} %get-tuple-element.651), channel_id=1, source_target_pairs={{4,0},{8,4},{12,8},{16,12},{20,16},{24,20},{28,24},{5,1},{9,5},{13... | collective-permute-start | bytes 786440 | tf_op jit(solution)/shard_map/while/body/eval_jaxpr/ppermute | solution.py:12
  (24 other events, 117.9 us)
where the time goes:
time: 254 us; the launch traced here: 253 us
  starting transfers between devices  92.3 us (36%)
  waiting for transfers between devices  54.4 us (21%)
  blocking collectives  44.9 us (18%)
  matrix products  43.7 us (17%)
  other arithmetic  8.44 us (3%)
  local copies, waits for them, and re-layouts  6.71 us (3%)
    ppermute x36, starting transfers between devices, from_behind(): lax.ppermute(value, axis, [(source, source + steps) for source in range(l...  92.3 us
    ppermute x36, waiting for transfers between devices, from_behind(): lax.ppermute(value, axis, [(source, source + steps) for source in range(l...  54.4 us
    psum x1, blocking collectives, local(): filter_total = lax.psum(local_terms, ('seq', 'tp'))  44.9 us
    conv_general_dilated x1, matrix products, local(): lax.conv_general_dilated(padded[None], mixed[:, None, :], (1,), 'VALID',...  11.7 us
    conv_general_dilated x1, matrix products, local(): lax.conv_general_dilated(padded[None], taps[:, None, :], (1,), 'VALID', d...  11.6 us
    dot_general x8, matrix products, query_tile(): jnp.einsum('hqk,khd->qhd', weights * (dprob - delta_heads[:, :, None]), k...  5.68 us
  transfers between devices with their start and end apart: 36, of which 21 were waited for; matrix products, arithmetic and copies ran while one was open for 11% of the time, Pallas kernels for 0%

commit v1 on v0

--- a/solution.py
+++ b/solution.py
@@ -1,6 +1,10 @@
+import functools
+
 import jax
 import jax.numpy as jnp
 from jax import lax
+from jax.experimental import pallas as pl
+from jax.experimental.pallas import tpu as pltpu
 from jax.sharding import PartitionSpec as P
 
 HEADS = 32
@@ -19,7 +23,7 @@
     return (high, low)
 
 
-def local(
+def local_ring(
     q_heads,
     k_heads,
     v_heads,
@@ -180,6 +184,533 @@
     return (grad_q, grad_k, grad_v, grad_gate, grad_feat_k, grad_feat_v, grad_filters)
 
 
+MESH = pl.DeviceIdType.MESH
+LANES = 128
+LOG2E = 1.4426950408889634
+
+
+def kernel(
+    n,
+    tp,
+    q_in,
+    k_in,
+    v_in,
+    do_in,
+    ao_in,
+    gate_in,
+    fk_in,
+    fv_in,
+    co_in,
+    gy_in,
+    taps,
+    gq_out,
+    gk_out,
+    gv_out,
+    gg_out,
+    gfk_out,
+    gfv_out,
+    gf_out,
+    heads_q,
+    heads_k,
+    heads_v,
+    heads_do,
+    keys_t,
+    delta_mine,
+    delta_all,
+    do_here,
+    ao_here,
+    gate,
+    fk,
+    fv,
+    co,
+    gy,
+    dz_here,
+    dz_rim,
+    dz_all,
+    terms,
+    partial_mine,
+    partial_in,
+    across,
+    scores,
+    acc_k,
+    acc_v,
+    res_q,
+    res_k,
+    res_v,
+    load_sem,
+    own_sem,
+    send_in,
+    recv_in,
+    send_rim,
+    recv_rim,
+    send_out,
+    recv_out,
+    own_out,
+    send_rs,
+    recv_rs,
+    send_tp,
+    recv_tp,
+    send_ag,
+    recv_ag,
+):
+    me = lax.axis_index("seq")
+    lane = lax.axis_index("tp")
+    rows, width = q_in.shape[0], q_in.shape[1] // n
+    channels = gy_in.shape[1]
+    span = taps.shape[0]
+    scale = 1.0 / width**0.5
+
+    loads = [
+        pltpu.make_async_copy(src, dst, load_sem.at[i])
+        for i, (src, dst) in enumerate(
+            (
+                (gy_in, gy),
+                (gate_in, gate),
+                (do_in, do_here),
+                (ao_in, ao_here),
+                (fk_in, fk),
+                (fv_in, fv),
+                (co_in, co),
+            )
+        )
+    ]
+    for load in loads:
+        load.start()
+
+    barrier = pltpu.get_barrier_semaphore()
+    for d in range(1, n):
+        pl.semaphore_signal(
+            barrier, inc=1, device_id={"seq": lax.rem(me + d, n)}, device_id_type=MESH
+        )
+    for d in range(1, tp):
+        pl.semaphore_signal(
+            barrier, inc=1, device_id={"tp": lax.rem(lane + d, tp)}, device_id_type=MESH
+        )
+    pl.semaphore_wait(barrier, n - 1 + tp - 1)
+
+    def cols(i):
+        return pl.ds(pl.multiple_of(i * width, width), width)
+
+    def block(i):
+        return pl.ds(pl.multiple_of(i * rows, rows), rows)
+
+    arrays = ((q_in, heads_q), (k_in, heads_k), (v_in, heads_v), (do_in, heads_do))
+    sends = []
+
+    def send_array(a):
+        src, dst = arrays[a]
+        own = pltpu.make_async_copy(src.at[:, cols(me)], dst.at[block(me), :], own_sem.at[a])
+        own.start()
+        sends.append((own, True))
+        for d in range(1, n):
+            peer = lax.rem(me + d, n)
+            copy = pltpu.make_async_remote_copy(
+                src_ref=src.at[:, cols(peer)],
+                dst_ref=dst.at[block(me), :],
+                send_sem=send_in.at[a, d],
+                recv_sem=recv_in.at[a, d],
+                device_id={"seq": peer},
+                device_id_type=MESH,
+            )
+            copy.start()
+            sends.append((copy, False))
+
+    send_array(0)
+    loads[0].wait()
+    loads[1].wait()
+    tiles = channels // LANES
+    for t in range(tiles):
+        at = slice(t * LANES, (t + 1) * LANES)
+        dz = (gy[:, at].astype(jnp.float32) * gate[:, at].astype(jnp.float32)).astype(jnp.bfloat16)
+        dz_here[:, at] = dz
+        dz_all[t, 0:rows, :] = dz.astype(jnp.float32)
+
+    def rim_copy():
+        return pltpu.make_async_remote_copy(
+            src_ref=dz_here,
+            dst_ref=dz_rim,
+            send_sem=send_rim,
+            recv_sem=recv_rim,
+            device_id={"seq": lax.rem(me + n - 1, n)},
+            device_id_type=MESH,
+        )
+
+    @pl.when(me > 0)
+    def _():
+        rim_copy().start()
+
+    send_array(1)
+    send_array(2)
+    send_array(3)
+
+    loads[2].wait()
+    loads[3].wait()
+    for h in range(n):
+        at = slice(h * width, (h + 1) * width)
+        prod = do_here[:, at].astype(jnp.float32) * ao_here[:, at].astype(jnp.float32)
+        line = jnp.sum(prod.T, axis=0, keepdims=True)
+        delta_mine[h] = jnp.broadcast_to(line, (8, rows))
+    delta_all[me] = delta_mine[me]
+    for d in range(1, n):
+        peer = lax.rem(me + d, n)
+        copy = pltpu.make_async_remote_copy(
+            src_ref=delta_mine.at[peer],
+            dst_ref=delta_all.at[me],
+            send_sem=send_in.at[4, d],
+            recv_sem=recv_in.at[4, d],
+            device_id={"seq": peer},
+            device_id_type=MESH,
+        )
+        copy.start()
+        sends.append((copy, False))
+
+    loads[4].wait()
+    loads[5].wait()
+    loads[6].wait()
+    for t in range(tiles):
+        at = slice(t * LANES, (t + 1) * LANES)
+        gg_out[:, at] = (gy[:, at].astype(jnp.float32) * co[:, at].astype(jnp.float32)).astype(
+            jnp.bfloat16
+        )
+    terms[...] = jnp.zeros_like(terms)
+
+    @pl.when(me < n - 1)
+    def _():
+        rim_copy().wait_recv()
+        for t in range(tiles):
+            at = slice(t * LANES, (t + 1) * LANES)
+            dz_all[t, rows : 2 * rows, :] = dz_rim[:, at].astype(jnp.float32)
+
+    @pl.when(me == n - 1)
+    def _():
+        for t in range(tiles):
+            dz_all[t, rows : 2 * rows, :] = jnp.zeros((rows, LANES), jnp.float32)
+
+    def conv_tile(t, carry):
+        at = pl.ds(pl.multiple_of(t * LANES, LANES), LANES)
+        left = fk[:, at].astype(jnp.float32)
+        right = fv[:, at].astype(jnp.float32)
+        mixed = left * right
+
+        def tap_step(step, acc):
+            base = pl.multiple_of(step * 8, 8)
+            for b in range(8):
+                x = dz_all[t, pl.ds(base + b, rows), :]
+                acc = acc + x * taps[pl.ds(base + b, 1), :]
+                folded = jnp.sum((x * mixed).reshape(rows // 8, 8, LANES), axis=0)
+                terms[base + b] = terms[base + b] + folded
+            return acc
+
+        acc = lax.fori_loop(0, span // 8, tap_step, jnp.zeros((rows, LANES), jnp.float32))
+        gfk_out[:, at] = (acc * right).astype(jnp.bfloat16)
+        gfv_out[:, at] = (acc * left).astype(jnp.bfloat16)
+        return carry
+
+    lax.fori_loop(0, tiles, conv_tile, 0)
+    per_lane = jnp.sum(terms[...], axis=1)
+    groups = gf_out.shape[0]
+    folded = per_lane
+    for g in range(1, LANES // groups):
+        folded = folded + pltpu.roll(per_lane, g * groups, 1)
+    share = groups // n
+    partial_mine[...] = folded.T[0:groups, :]
+
+    def slab(i):
+        return pl.ds(pl.multiple_of(i * share, share), share)
+
+    partial_in[me] = partial_mine[slab(me), :]
+    small = []
+    for d in range(1, n):
+        peer = lax.rem(me + d, n)
+        copy = pltpu.make_async_remote_copy(
+            src_ref=partial_mine.at[slab(peer), :],
+            dst_ref=partial_in.at[me],
+            send_sem=send_rs.at[d],
+            recv_sem=recv_rs.at[d],
+            device_id={"seq": peer},
+            device_id_type=MESH,
+        )
+        copy.start()
+        small.append(copy)
+
+    for copy, is_local in sends:
+        if is_local:
+            copy.wait()
+        else:
+            copy.wait_recv()
+    for copy in small:
+        copy.wait_recv()
+    total = partial_in[0]
+    for i in range(1, n):
+        total = total + partial_in[i]
+    across[lane] = total
+    crossing = []
+    for d in range(1, tp):
+        copy = pltpu.make_async_remote_copy(
+            src_ref=across.at[lane],
+            dst_ref=across.at[lane],
+            send_sem=send_tp.at[d],
+            recv_sem=recv_tp.at[d],
+            device_id={"tp": lax.rem(lane + d, tp)},
+            device_id_type=MESH,
+        )
+        copy.start()
+        crossing.append(copy)
+
+    tile = 2 * rows
+    steps = n * rows // tile
+    for j in range(steps):
+        at = slice(j * tile, (j + 1) * tile)
+        keys_t[:, at] = heads_k[at, :].T
+    acc_k[...] = jnp.zeros_like(acc_k)
+    acc_v[...] = jnp.zeros_like(acc_v)
+    key_id = lax.broadcasted_iota(jnp.int32, (tile, tile), 0)
+    query_id = lax.broadcasted_iota(jnp.int32, (tile, tile), 1)
+    nt = (((1,), (1,)), ((), ()))
+    nn = (((1,), (0,)), ((), ()))
+
+    def dot(a, b, dims):
+        return lax.dot_general(a, b, dims, preferred_element_type=jnp.float32)
+
+    results = ((res_q, gq_out), (res_k, gk_out), (res_v, gv_out))
+
+    def out_copy(a, r, src_rows):
+        src, dst = results[a]
+        return pltpu.make_async_remote_copy(
+            src_ref=src.at[src_rows, :],
+            dst_ref=dst.at[:, cols(me)],
+            send_sem=send_out.at[a, r],
+            recv_sem=recv_out.at[a, me],
+            device_id={"seq": r},
+            device_id_type=MESH,
+        )
+
+    def own_copy(a, r):
+        src, dst = results[a]
+        return pltpu.make_async_copy(src.at[block(r), :], dst.at[:, cols(me)], own_out.at[a])
+
+    for i in reversed(range(steps)):
+        at_q = slice(i * tile, (i + 1) * tile)
+        query = heads_q[at_q, :]
+        upstream = heads_do[at_q, :]
+        delta = jnp.concatenate(
+            [delta_all[2 * i][0:1, :], delta_all[2 * i + 1][0:1, :]], axis=1
+        )
+        top = None
+        for j in range(i + 1):
+            at_k = slice(j * tile, (j + 1) * tile)
+            raw = dot(heads_k[at_k, :], query, nt)
+            if j == i:
+                raw = jnp.where(key_id <= query_id, raw, -1e30)
+            scores[at_k, :] = raw
+            high = jnp.max(raw, axis=0, keepdims=True)
+            top = high if top is None else jnp.maximum(top, high)
+        total = jnp.zeros_like(top)
+        for j in range(i + 1):
+            at_k = slice(j * tile, (j + 1) * tile)
+            weight = jnp.exp2((scores[at_k, :] - top) * (scale * LOG2E))
+            scores[at_k, :] = weight
+            total = total + jnp.sum(weight, axis=0, keepdims=True)
+        lse = top * scale + jnp.log(total)
+        lse_high = lse.astype(jnp.bfloat16).astype(jnp.float32)
+        lse_w = lse_high + (lse - lse_high).astype(jnp.bfloat16).astype(jnp.float32)
+        delta_high = delta.astype(jnp.bfloat16).astype(jnp.float32)
+        delta_w = delta_high + (delta - delta_high).astype(jnp.bfloat16).astype(jnp.float32)
+        share_q = 1.0 / total
+        share_k = share_q * jnp.exp(lse - lse_w)
+        grad_t = jnp.zeros((width, tile), jnp.float32)
+        for j in range(i + 1):
+            at_k = slice(j * tile, (j + 1) * tile)
+            weight = scores[at_k, :]
+            dprob = dot(heads_v[at_k, :], upstream, nt)
+            dscore = (weight * share_q) * (dprob - delta)
+            probs_k = weight * share_k
+            dscore_k = (probs_k * (dprob - delta_w)).astype(jnp.bfloat16)
+            big = dscore.astype(jnp.bfloat16)
+            rest = (dscore - big.astype(jnp.float32)).astype(jnp.bfloat16)
+            grad_t = grad_t + dot(keys_t[:, at_k], big, nn) + dot(keys_t[:, at_k], rest, nn)
+            acc_v[at_k, :] = acc_v[at_k, :] + dot(probs_k.astype(jnp.bfloat16), upstream, nn)
+            acc_k[at_k, :] = acc_k[at_k, :] + dot(dscore_k, query, nn)
+        res_q[at_q, :] = (grad_t * scale).T.astype(jnp.bfloat16)
+        res_k[at_q, :] = (acc_k[at_q, :] * scale).astype(jnp.bfloat16)
+        res_v[at_q, :] = acc_v[at_q, :].astype(jnp.bfloat16)
+        for r in (2 * i, 2 * i + 1):
+
+            @pl.when(me != r)
+            def _():
+                for a in range(3):
+                    out_copy(a, r, slice(r * rows, (r + 1) * rows)).start()
+
+            @pl.when(me == r)
+            def _():
+                for a in range(3):
+                    own_copy(a, r).start()
+
+    for copy in crossing:
+        copy.wait_recv()
+    total = across[0]
+    for i in range(1, tp):
+        total = total + across[i]
+    count_all = rows * n * channels * tp / groups
+    gf_out[slab(me), :] = total * (1.0 / count_all**0.5)
+    gather = []
+    for d in range(1, n):
+        copy = pltpu.make_async_remote_copy(
+            src_ref=gf_out.at[slab(me), :],
+            dst_ref=gf_out.at[slab(me), :],
+            send_sem=send_ag.at[d],
+            recv_sem=recv_ag.at[d],
+            device_id={"seq": lax.rem(me + d, n)},
+            device_id_type=MESH,
+        )
+        copy.start()
+        gather.append(copy)
+
+    for copy, is_local in sends:
+        if not is_local:
+            copy.wait_send()
+    for copy in small + crossing:
+        copy.wait_send()
+
+    @pl.when(me > 0)
+    def _():
+        rim_copy().wait_send()
+
+    for r in range(n):
+
+        @pl.when(me != r)
+        def _():
+            for a in range(3):
+                out_copy(a, r, slice(r * rows, (r + 1) * rows)).wait_send()
+
+    for a in range(3):
+        own_copy(a, me).wait()
+        for d in range(1, n):
+            peer = lax.rem(me + d, n)
+            src, dst = results[a]
+            pltpu.make_async_remote_copy(
+                src_ref=src.at[block(me), :],
+                dst_ref=dst.at[:, cols(peer)],
+                send_sem=send_out.at[a, peer],
+                recv_sem=recv_out.at[a, peer],
+                device_id={"seq": peer},
+                device_id_type=MESH,
+            ).wait_recv()
+    for copy in gather:
+        copy.wait()
+
+
+def local_heads(
+    n,
+    tp,
+    q_heads,
+    k_heads,
+    v_heads,
+    grad_attn,
+    attn_out,
+    gate_q,
+    feat_k,
+    feat_v,
+    conv_out,
+    grad_y,
+    filters,
+):
+    rows, wide = q_heads.shape
+    width = wide // n
+    channels = gate_q.shape[1]
+    groups, span = filters.shape
+    taps = jnp.tile(filters.T, (1, LANES // groups))
+    share = groups // n
+    tiles = channels // LANES
+    bf16, f32 = (jnp.bfloat16, jnp.float32)
+    anywhere = pl.BlockSpec(memory_space=pl.ANY)
+    inside = pl.BlockSpec(memory_space=pltpu.VMEM)
+    dma = pltpu.SemaphoreType.DMA
+    return pl.pallas_call(
+        functools.partial(kernel, n, tp),
+        out_shape=(
+            [jax.ShapeDtypeStruct((rows, wide), bf16)] * 3
+            + [jax.ShapeDtypeStruct((rows, channels), bf16)] * 3
+            + [jax.ShapeDtypeStruct((groups, span), f32)]
+        ),
+        in_specs=[anywhere] * 10 + [inside],
+        out_specs=[anywhere] * 3 + [inside] * 4,
+        scratch_shapes=(
+            [pltpu.VMEM((n * rows, width), bf16)] * 4
+            + [
+                pltpu.VMEM((width, n * rows), bf16),
+                pltpu.VMEM((n, 8, rows), f32),
+                pltpu.VMEM((n, 8, rows), f32),
+            ]
+            + [pltpu.VMEM((rows, wide), bf16)] * 2
+            + [pltpu.VMEM((rows, channels), bf16)] * 7
+            + [
+                pltpu.VMEM((tiles, 2 * rows, LANES), f32),
+                pltpu.VMEM((span, 8, LANES), f32),
+                pltpu.VMEM((groups, span), f32),
+                pltpu.VMEM((n, share, span), f32),
+                pltpu.VMEM((tp, share, span), f32),
+                pltpu.VMEM((n * rows, 2 * rows), f32),
+            ]
+            + [pltpu.VMEM((n * rows, width), f32)] * 2
+            + [pltpu.VMEM((n * rows, width), bf16)] * 3
+            + [
+                dma((7,)),
+                dma((4,)),
+                dma((5, n)),
+                dma((5, n)),
+                dma,
+                dma,
+                dma((3, n)),
+                dma((3, n)),
+                dma((3,)),
+                dma((n,)),
+                dma((n,)),
+                dma((tp,)),
+                dma((tp,)),
+                dma((n,)),
+                dma((n,)),
+            ]
+        ),
+        compiler_params=pltpu.CompilerParams(
+            collective_id=0, has_side_effects=True, vmem_limit_bytes=48 * 1024 * 1024
+        ),
+    )(
+        q_heads,
+        k_heads,
+        v_heads,
+        grad_attn,
+        attn_out,
+        gate_q,
+        feat_k,
+        feat_v,
+        conv_out,
+        grad_y,
+        taps,
+    )
+
+
+def local(*args):
+    n, tp = (lax.axis_size("seq"), lax.axis_size("tp"))
+    rows, wide = args[0].shape
+    groups, span = args[10].shape
+    fits = (
+        HEADS // tp == n
+        and n > 1
+        and tp > 1
+        and n % 2 == 0
+        and rows == LANES
+        and wide == n * LANES
+        and span <= rows
+        and span == LANES
+        and LANES % groups == 0
+        and groups % (8 * n) == 0
+    )
+    if fits:
+        return tuple(local_heads(n, tp, *args))
+    return local_ring(*args)
+
+
 def solution(mesh):
     in_specs = (
         P("seq", "tp"),

time: 254 us -> 101 us (0.40)
  starting transfers between devices: 92.3 us -> 0 us
  Pallas kernels: 0 us -> 84.5 us
  waiting for transfers between devices: 54.4 us -> 0 us
  blocking collectives: 44.9 us -> 0 us
  matrix products: 43.7 us -> 0 us
  other arithmetic: 8.44 us -> 0 us
  local copies, waits for them, and re-layouts: 6.71 us -> 14.9 us
    ppermute x36 -> x0, starting transfers between devices: 92.3 us -> none  [from_behind(): lax.ppermute(value, axis, [(source, source + steps) for source in range(l...]
    pallas_call x0 -> x1, Pallas kernels: none -> 84.5 us  [local_heads(): pl.pallas_call(functools.partial(kernel, n, tp), out_shape=[jax.ShapeDtyp...]
    ppermute x36 -> x0, waiting for transfers between devices: 54.4 us -> none  [from_behind(): lax.ppermute(value, axis, [(source, source + steps) for source in range(l...]
    psum x1 -> x0, blocking collectives: 44.9 us -> none  [local(): filter_total = lax.psum(local_terms, ('seq', 'tp'))]
    conv_general_dilated x2 -> x0, matrix products: 23.2 us -> none  [the longest x1 11.7 us: local(): lax.conv_general_dilated(padded[None], mixed[:, None, :], (1,), 'VALID',...]
    dot_general x47 -> x0, matrix products: 20.5 us -> none  [the longest x8 5.68 us: query_tile(): jnp.einsum('hqk,khd->qhd', weights * (dprob - delta_heads[:, :, None]), k...]
    unnamed x30 -> x25, local copies, waits for them, and re-layouts: 2.06 us -> 14 us
    convert_element_type x5 -> x0, other arithmetic: 4.28 us -> none  [the longest x1 2.69 us: local(): (grad_y.astype(jnp.float32) * gate_q.astype(jnp.float32)).astype(jnp.bflo...]
  transfers between devices with their start and end apart: 36 -> 0, of which waited for: 21 -> 0; matrix products, arithmetic and copies ran while one was open for 11% -> 0% of each run, Pallas kernels for 0% -> 0%
where the time goes in v1:
time: 101 us; the launch traced here: 100 us
  Pallas kernels  84.5 us (84%)
  local copies, waits for them, and re-layouts  14.9 us (15%)
    pallas_call x1, Pallas kernels, local_heads(): pl.pallas_call(functools.partial(kernel, n, tp), out_shape=[jax.ShapeDtyp...  84.5 us
    unnamed x25, local copies, waits for them, and re-layouts  14 us

profile of v1, /device:TPU:0, one launch (start us, length us, event | category | flops | bytes accessed | tf_op | source)
XLA Modules:
  0.0 100.1 jit_solution(7204406663175156092)
XLA Ops:
  0.6 0.8 tile.4
  1.4 0.1 copy.19.taps
  1.5 0.0 copy-start
  1.5 1.0 %copy-done = bf16[128,2048]{1,0:T(8,128)(2,1)S(1)} copy-done((bf16[128,2048]{1,0:T(8,128)(2,1)S(1)}, bf16[128,2048]{1,0:T(8,128)(2,1)}, u32[]{:S(2)}) %copy-start) | copy-done | bytes 524312
  2.5 0.0 copy-start.1
  2.5 1.0 %copy-done.1 = bf16[128,2048]{1,0:T(8,128)(2,1)S(1)} copy-done((bf16[128,2048]{1,0:T(8,128)(2,1)S(1)}, bf16[128,2048]{1,0:T(8,128)(2,1)}, u32[]{:S(2)}) %copy-start.1) | copy-done | bytes 524312
  3.6 0.0 copy-start.2
  3.6 1.0 %copy-done.2 = bf16[128,2048]{1,0:T(8,128)(2,1)S(1)} copy-done((bf16[128,2048]{1,0:T(8,128)(2,1)S(1)}, bf16[128,2048]{1,0:T(8,128)(2,1)}, u32[]{:S(2)}) %copy-start.2) | copy-done | bytes 524312
  4.6 0.0 copy-start.3
  4.6 1.0 %copy-done.3 = bf16[128,2048]{1,0:T(8,128)(2,1)S(1)} copy-done((bf16[128,2048]{1,0:T(8,128)(2,1)S(1)}, bf16[128,2048]{1,0:T(8,128)(2,1)}, u32[]{:S(2)}) %copy-start.3) | copy-done | bytes 524312
  5.7 0.0 copy-start.4
  5.7 0.9 copy-done.4
  6.6 0.9 copy-done.5
  7.6 0.9 copy-done.6
  8.5 0.9 copy-done.7
  9.5 0.9 copy-done.8
  10.4 84.5 %shard_map.162 = (bf16[128,1024]{1,0:T(8,128)(2,1)S(1)}, bf16[128,1024]{1,0:T(8,128)(2,1)S(1)}, bf16[128,1024]{1,0:T(8,128)(2,1)S(1)}, bf16[128,2048]{1,0:T(8,12...) custom-call(bf16[128,1024]{1,0:T(8,128)(2,1)S(1)} %copy-done.4, ...), custom_call_target="tpu_custom_call" | custom-call | tf_op jit(solution)/shard_map/pallas_call | solution.py:629
  95.0 0.7 copy.27
  95.7 0.7 copy.28
  96.4 0.7 copy.29
  97.1 0.8 copy.30
  97.9 0.8 copy.31
  98.7 0.8 copy.32
  99.5 0.6 copy.33
  (4 shorter events, 0.0 us)
Async XLA Ops:
  1.5 1.0 %copy-start = (bf16[128,2048]{1,0:T(8,128)(2,1)S(1)}, bf16[128,2048]{1,0:T(8,128)(2,1)}, u32[]{:S(2)}) copy-start(bf16[128,2048]{1,0:T(8,128)(2,1)} %gate_in.1) | copy-start | bytes 1572868
  2.5 1.0 %copy-start.1 = (bf16[128,2048]{1,0:T(8,128)(2,1)S(1)}, bf16[128,2048]{1,0:T(8,128)(2,1)}, u32[]{:S(2)}) copy-start(bf16[128,2048]{1,0:T(8,128)(2,1)} %fk_in.1) | copy-start | bytes 1572868
  3.6 1.0 %copy-start.2 = (bf16[128,2048]{1,0:T(8,128)(2,1)S(1)}, bf16[128,2048]{1,0:T(8,128)(2,1)}, u32[]{:S(2)}) copy-start(bf16[128,2048]{1,0:T(8,128)(2,1)} %fv_in.1) | copy-start | bytes 1572868
  4.6 1.0 %copy-start.3 = (bf16[128,2048]{1,0:T(8,128)(2,1)S(1)}, bf16[128,2048]{1,0:T(8,128)(2,1)}, u32[]{:S(2)}) copy-start(bf16[128,2048]{1,0:T(8,128)(2,1)} %co_in.1) | copy-start | bytes 1572868
  5.7 0.9 copy-start.4
  6.6 0.9 copy-start.5
  7.6 0.9 copy-start.6
  8.5 0.9 copy-start.7
  9.5 0.9 copy-start.8

commit v2 on v1

--- a/solution.py
+++ b/solution.py
@@ -202,7 +202,7 @@
     fv_in,
     co_in,
     gy_in,
-    taps,
+    filters,
     gq_out,
     gk_out,
     gv_out,
@@ -227,6 +227,7 @@
     dz_here,
     dz_rim,
     dz_all,
+    taps,
     terms,
     partial_mine,
     partial_in,
@@ -257,7 +258,7 @@
     lane = lax.axis_index("tp")
     rows, width = q_in.shape[0], q_in.shape[1] // n
     channels = gy_in.shape[1]
-    span = taps.shape[0]
+    span = filters.shape[1]
     scale = 1.0 / width**0.5
 
     loads = [
@@ -296,12 +297,10 @@
 
     arrays = ((q_in, heads_q), (k_in, heads_k), (v_in, heads_v), (do_in, heads_do))
     sends = []
-
-    def send_array(a):
-        src, dst = arrays[a]
+    for a, (src, dst) in enumerate(arrays):
         own = pltpu.make_async_copy(src.at[:, cols(me)], dst.at[block(me), :], own_sem.at[a])
         own.start()
-        sends.append((own, True))
+        sends.append((0, own))
         for d in range(1, n):
             peer = lax.rem(me + d, n)
             copy = pltpu.make_async_remote_copy(
@@ -312,10 +311,16 @@
                 device_id={"seq": peer},
                 device_id_type=MESH,
             )
-            copy.start()
-            sends.append((copy, False))
-
-    send_array(0)
+            sends.append((d, copy))
+
+    def start_sends(later):
+        for d, copy in sends:
+            if d > 0:
+
+                @pl.when(me + d < n if later else me + d >= n)
+                def _():
+                    copy.start()
+
     loads[0].wait()
     loads[1].wait()
     tiles = channels // LANES
@@ -339,9 +344,7 @@
     def _():
         rim_copy().start()
 
-    send_array(1)
-    send_array(2)
-    send_array(3)
+    start_sends(True)
 
     loads[2].wait()
     loads[3].wait()
@@ -351,6 +354,7 @@
         line = jnp.sum(prod.T, axis=0, keepdims=True)
         delta_mine[h] = jnp.broadcast_to(line, (8, rows))
     delta_all[me] = delta_mine[me]
+    deltas = []
     for d in range(1, n):
         peer = lax.rem(me + d, n)
         copy = pltpu.make_async_remote_copy(
@@ -362,7 +366,7 @@
             device_id_type=MESH,
         )
         copy.start()
-        sends.append((copy, False))
+        deltas.append(copy)
 
     loads[4].wait()
     loads[5].wait()
@@ -373,6 +377,8 @@
             jnp.bfloat16
         )
     terms[...] = jnp.zeros_like(terms)
+    both = jnp.concatenate([filters[...]] * (LANES // filters.shape[0]), axis=0)
+    taps[...] = both.T
 
     @pl.when(me < n - 1)
     def _():
@@ -385,6 +391,12 @@
     def _():
         for t in range(tiles):
             dz_all[t, rows : 2 * rows, :] = jnp.zeros((rows, LANES), jnp.float32)
+
+    @pl.when(me > 0)
+    def _():
+        rim_copy().wait_send()
+
+    start_sends(False)
 
     def conv_tile(t, carry):
         at = pl.ds(pl.multiple_of(t * LANES, LANES), LANES)
@@ -433,11 +445,13 @@
         copy.start()
         small.append(copy)
 
-    for copy, is_local in sends:
-        if is_local:
+    for d, copy in sends:
+        if d == 0:
             copy.wait()
         else:
             copy.wait_recv()
+    for copy in deltas:
+        copy.wait_recv()
     for copy in small:
         copy.wait_recv()
     total = partial_in[0]
@@ -566,15 +580,11 @@
         copy.start()
         gather.append(copy)
 
-    for copy, is_local in sends:
-        if not is_local:
+    for d, copy in sends:
+        if d > 0:
             copy.wait_send()
-    for copy in small + crossing:
+    for copy in deltas + small + crossing:
         copy.wait_send()
-
-    @pl.when(me > 0)
-    def _():
-        rim_copy().wait_send()
 
     for r in range(n):
 
@@ -619,7 +629,6 @@
     width = wide // n
     channels = gate_q.shape[1]
     groups, span = filters.shape
-    taps = jnp.tile(filters.T, (1, LANES // groups))
     share = groups // n
     tiles = channels // LANES
     bf16, f32 = (jnp.bfloat16, jnp.float32)
@@ -646,6 +655,7 @@
             + [pltpu.VMEM((rows, channels), bf16)] * 7
             + [
                 pltpu.VMEM((tiles, 2 * rows, LANES), f32),
+                pltpu.VMEM((span, LANES), f32),
                 pltpu.VMEM((span, 8, LANES), f32),
                 pltpu.VMEM((groups, span), f32),
                 pltpu.VMEM((n, share, span), f32),
@@ -673,7 +683,7 @@
             ]
         ),
         compiler_params=pltpu.CompilerParams(
-            collective_id=0, has_side_effects=True, vmem_limit_bytes=48 * 1024 * 1024
+            collective_id=0, has_side_effects=True, vmem_limit_bytes=67043328
         ),
     )(
         q_heads,
@@ -686,7 +696,7 @@
         feat_v,
         conv_out,
         grad_y,
-        taps,
+        filters,
     )
 
 

time: 101 us -> 81.2 us (0.80)
  Pallas kernels: 84.5 us -> 73.2 us
  local copies, waits for them, and re-layouts: 14.9 us -> 7.01 us
    pallas_call x1, Pallas kernels: 84.5 us -> 73.2 us  [local_heads(): pl.pallas_call(functools.partial(kernel, n, tp), out_shape=[jax.ShapeDtyp...]
    unnamed x25 -> x19, local copies, waits for them, and re-layouts: 14 us -> 7.01 us
where the time goes in v2:
time: 81.2 us; the launch traced here: 80.9 us
  Pallas kernels  73.2 us (90%)
  local copies, waits for them, and re-layouts  7.01 us (9%)
    pallas_call x1, Pallas kernels, local_heads(): pl.pallas_call(functools.partial(kernel, n, tp), out_shape=[jax.ShapeDtyp...  73.2 us
    unnamed x19, local copies, waits for them, and re-layouts  7.01 us

profile of v2, /device:TPU:0, one launch (start us, length us, event | category | flops | bytes accessed | tf_op | source)
XLA Modules:
  0.0 80.9 jit_solution(13488571910566005672)
XLA Ops:
  0.6 73.2 %shard_map.162 = (bf16[128,1024]{1,0:T(8,128)(2,1)}, bf16[128,1024]{1,0:T(8,128)(2,1)}, bf16[128,1024]{1,0:T(8,128)(2,1)}, bf16[128,2048]{1,0:T(8,128)(2,1)}, bf...) custom-call(bf16[128,1024]{1,0:T(8,128)(2,1)} %q_in.1, bf16[128,1024]{1,0:T(8,128)(2,1)} %k_in.1, ...), custom_call_target="tpu_custom_call" | custom-call | tf_op jit(solution)/shard_map/pallas_call | solution.py:638
  73.9 0.0 copy-start.4
  73.9 0.0 copy-start.3
  73.9 1.7 %copy.25 = bf16[128,1024]{1,0:T(8,128)(2,1)} copy(bf16[128,1024]{1,0:T(8,128)(2,1)} %get-tuple-element.14) | data formatting | bytes 524288
  75.6 0.0 copy-done.4
  75.6 0.0 copy-start.2
  75.6 0.7 copy.26
  76.3 0.0 copy-done.3
  76.3 0.7 copy.27
  77.0 0.0 copy-done.2
  77.0 0.0 copy-start.1
  77.0 0.8 copy.28
  77.8 0.4 copy-done.1
  78.2 0.0 copy-start
  78.3 0.8 copy.29
  79.0 0.4 copy-done
  79.5 0.0 copy-start.5
  79.5 0.8 copy.30
  80.3 0.0 copy-done.5
  80.3 0.6 copy.31
Async XLA Ops:
  73.9 1.7 %copy-start.4 = (bf16[128,1024]{1,0:T(8,128)(2,1)S(1)}, bf16[128,1024]{1,0:T(8,128)(2,1)}, u32[]{:S(2)}) copy-start(bf16[128,1024]{1,0:T(8,128)(2,1)} %get-tuple-element.15) | copy-start | bytes 786436
  73.9 2.4 %copy-start.3 = (bf16[128,1024]{1,0:T(8,128)(2,1)S(1)}, bf16[128,1024]{1,0:T(8,128)(2,1)}, u32[]{:S(2)}) copy-start(bf16[128,1024]{1,0:T(8,128)(2,1)} %get-tuple-element.16) | copy-start | bytes 786436
  75.6 1.4 %copy-start.2 = (bf16[128,2048]{1,0:T(8,128)(2,1)S(1)}, bf16[128,2048]{1,0:T(8,128)(2,1)}, u32[]{:S(2)}) copy-start(bf16[128,2048]{1,0:T(8,128)(2,1)} %get-tuple-element.17) | copy-start | bytes 1572868
  77.0 1.2 %copy-start.1 = (bf16[128,2048]{1,0:T(8,128)(2,1)S(1)}, bf16[128,2048]{1,0:T(8,128)(2,1)}, u32[]{:S(2)}) copy-start(bf16[128,2048]{1,0:T(8,128)(2,1)} %get-tuple-element.18) | copy-start | bytes 1572868
  78.2 1.2 %copy-start = (bf16[128,2048]{1,0:T(8,128)(2,1)S(1)}, bf16[128,2048]{1,0:T(8,128)(2,1)}, u32[]{:S(2)}) copy-start(bf16[128,2048]{1,0:T(8,128)(2,1)} %get-tuple-element.19) | copy-start | bytes 1572868
  79.5 0.8 copy-start.5

commit v3 on v2

--- a/solution.py
+++ b/solution.py
@@ -227,6 +227,8 @@
     dz_here,
     dz_rim,
     dz_all,
+    rim_all,
+    dw_all,
     taps,
     terms,
     partial_mine,
@@ -313,14 +315,6 @@
             )
             sends.append((d, copy))
 
-    def start_sends(later):
-        for d, copy in sends:
-            if d > 0:
-
-                @pl.when(me + d < n if later else me + d >= n)
-                def _():
-                    copy.start()
-
     loads[0].wait()
     loads[1].wait()
     tiles = channels // LANES
@@ -329,6 +323,7 @@
         dz = (gy[:, at].astype(jnp.float32) * gate[:, at].astype(jnp.float32)).astype(jnp.bfloat16)
         dz_here[:, at] = dz
         dz_all[t, 0:rows, :] = dz.astype(jnp.float32)
+        dz_all[t, rows : rows + 8, :] = jnp.zeros((8, LANES), jnp.float32)
 
     def rim_copy():
         return pltpu.make_async_remote_copy(
@@ -344,7 +339,10 @@
     def _():
         rim_copy().start()
 
-    start_sends(True)
+    for d, copy in sends:
+        if d > 0:
+            copy.start()
+
 
     loads[2].wait()
     loads[3].wait()
@@ -380,70 +378,26 @@
     both = jnp.concatenate([filters[...]] * (LANES // filters.shape[0]), axis=0)
     taps[...] = both.T
 
-    @pl.when(me < n - 1)
-    def _():
-        rim_copy().wait_recv()
-        for t in range(tiles):
-            at = slice(t * LANES, (t + 1) * LANES)
-            dz_all[t, rows : 2 * rows, :] = dz_rim[:, at].astype(jnp.float32)
-
-    @pl.when(me == n - 1)
-    def _():
-        for t in range(tiles):
-            dz_all[t, rows : 2 * rows, :] = jnp.zeros((rows, LANES), jnp.float32)
-
-    @pl.when(me > 0)
-    def _():
-        rim_copy().wait_send()
-
-    start_sends(False)
-
-    def conv_tile(t, carry):
+    def conv_own(t, carry):
         at = pl.ds(pl.multiple_of(t * LANES, LANES), LANES)
-        left = fk[:, at].astype(jnp.float32)
-        right = fv[:, at].astype(jnp.float32)
-        mixed = left * right
-
-        def tap_step(step, acc):
-            base = pl.multiple_of(step * 8, 8)
+        mixed = fk[:, at].astype(jnp.float32) * fv[:, at].astype(jnp.float32)
+        for a in range(span // 8):
+            size = rows - 8 * a
+            part = None
             for b in range(8):
-                x = dz_all[t, pl.ds(base + b, rows), :]
-                acc = acc + x * taps[pl.ds(base + b, 1), :]
-                folded = jnp.sum((x * mixed).reshape(rows // 8, 8, LANES), axis=0)
-                terms[base + b] = terms[base + b] + folded
-            return acc
-
-        acc = lax.fori_loop(0, span // 8, tap_step, jnp.zeros((rows, LANES), jnp.float32))
-        gfk_out[:, at] = (acc * right).astype(jnp.bfloat16)
-        gfv_out[:, at] = (acc * left).astype(jnp.bfloat16)
+                tap = 8 * a + b
+                x = dz_all[t, tap : tap + size, :]
+                term = x * taps[tap : tap + 1, :]
+                part = term if part is None else part + term
+                prod = (x * mixed[0:size]).reshape(size // 8, 8, LANES)
+                terms[tap] = terms[tap] + jnp.sum(prod, axis=0)
+            if a == 0:
+                dw_all[t] = part
+            else:
+                dw_all[t, 0:size, :] = dw_all[t, 0:size, :] + part
         return carry
 
-    lax.fori_loop(0, tiles, conv_tile, 0)
-    per_lane = jnp.sum(terms[...], axis=1)
-    groups = gf_out.shape[0]
-    folded = per_lane
-    for g in range(1, LANES // groups):
-        folded = folded + pltpu.roll(per_lane, g * groups, 1)
-    share = groups // n
-    partial_mine[...] = folded.T[0:groups, :]
-
-    def slab(i):
-        return pl.ds(pl.multiple_of(i * share, share), share)
-
-    partial_in[me] = partial_mine[slab(me), :]
-    small = []
-    for d in range(1, n):
-        peer = lax.rem(me + d, n)
-        copy = pltpu.make_async_remote_copy(
-            src_ref=partial_mine.at[slab(peer), :],
-            dst_ref=partial_in.at[me],
-            send_sem=send_rs.at[d],
-            recv_sem=recv_rs.at[d],
-            device_id={"seq": peer},
-            device_id_type=MESH,
-        )
-        copy.start()
-        small.append(copy)
+    lax.fori_loop(0, tiles, conv_own, 0)
 
     for d, copy in sends:
         if d == 0:
@@ -452,25 +406,6 @@
             copy.wait_recv()
     for copy in deltas:
         copy.wait_recv()
-    for copy in small:
-        copy.wait_recv()
-    total = partial_in[0]
-    for i in range(1, n):
-        total = total + partial_in[i]
-    across[lane] = total
-    crossing = []
-    for d in range(1, tp):
-        copy = pltpu.make_async_remote_copy(
-            src_ref=across.at[lane],
-            dst_ref=across.at[lane],
-            send_sem=send_tp.at[d],
-            recv_sem=recv_tp.at[d],
-            device_id={"tp": lax.rem(lane + d, tp)},
-            device_id_type=MESH,
-        )
-        copy.start()
-        crossing.append(copy)
-
     tile = 2 * rows
     steps = n * rows // tile
     for j in range(steps):
@@ -560,6 +495,86 @@
                 for a in range(3):
                     own_copy(a, r).start()
 
+    @pl.when(me < n - 1)
+    def _():
+        rim_copy().wait_recv()
+        for t in range(tiles):
+            at = slice(t * LANES, (t + 1) * LANES)
+            rim_all[t, 0:8, :] = jnp.zeros((8, LANES), jnp.float32)
+            rim_all[t, 8 : rows + 8, :] = dz_rim[:, at].astype(jnp.float32)
+
+    @pl.when(me == n - 1)
+    def _():
+        for t in range(tiles):
+            rim_all[t, 0 : rows + 8, :] = jnp.zeros((rows + 8, LANES), jnp.float32)
+
+    def conv_rim(t, carry):
+        at = pl.ds(pl.multiple_of(t * LANES, LANES), LANES)
+        left = fk[:, at].astype(jnp.float32)
+        right = fv[:, at].astype(jnp.float32)
+        mixed = left * right
+        for a in range(span // 8):
+            size = 8 * (a + 1)
+            part = None
+            for b in range(8):
+                tap = 8 * a + b
+                x = rim_all[t, b : b + size, :]
+                term = x * taps[tap : tap + 1, :]
+                part = term if part is None else part + term
+                prod = (x * mixed[rows - size : rows]).reshape(size // 8, 8, LANES)
+                terms[tap] = terms[tap] + jnp.sum(prod, axis=0)
+            dw_all[t, rows - size : rows, :] = dw_all[t, rows - size : rows, :] + part
+        acc = dw_all[t]
+        gfk_out[:, at] = (acc * right).astype(jnp.bfloat16)
+        gfv_out[:, at] = (acc * left).astype(jnp.bfloat16)
+        return carry
+
+    lax.fori_loop(0, tiles, conv_rim, 0)
+    per_lane = jnp.sum(terms[...], axis=1)
+    groups = gf_out.shape[0]
+    folded = per_lane
+    for g in range(1, LANES // groups):
+        folded = folded + pltpu.roll(per_lane, g * groups, 1)
+    share = groups // n
+    partial_mine[...] = folded.T[0:groups, :]
+
+    def slab(i):
+        return pl.ds(pl.multiple_of(i * share, share), share)
+
+    partial_in[me] = partial_mine[slab(me), :]
+    small = []
+    for d in range(1, n):
+        peer = lax.rem(me + d, n)
+        copy = pltpu.make_async_remote_copy(
+            src_ref=partial_mine.at[slab(peer), :],
+            dst_ref=partial_in.at[me],
+            send_sem=send_rs.at[d],
+            recv_sem=recv_rs.at[d],
+            device_id={"seq": peer},
+            device_id_type=MESH,
+        )
+        copy.start()
+        small.append(copy)
+
+    for copy in small:
+        copy.wait_recv()
+    total = partial_in[0]
+    for i in range(1, n):
+        total = total + partial_in[i]
+    across[lane] = total
+    crossing = []
+    for d in range(1, tp):
+        copy = pltpu.make_async_remote_copy(
+            src_ref=across.at[lane],
+            dst_ref=across.at[lane],
+            send_sem=send_tp.at[d],
+            recv_sem=recv_tp.at[d],
+            device_id={"tp": lax.rem(lane + d, tp)},
+            device_id_type=MESH,
+        )
+        copy.start()
+        crossing.append(copy)
+
     for copy in crossing:
         copy.wait_recv()
     total = across[0]
@@ -579,6 +594,10 @@
         )
         copy.start()
         gather.append(copy)
+
+    @pl.when(me > 0)
+    def _():
+        rim_copy().wait_send()
 
     for d, copy in sends:
         if d > 0:
@@ -654,7 +673,9 @@
             + [pltpu.VMEM((rows, wide), bf16)] * 2
             + [pltpu.VMEM((rows, channels), bf16)] * 7
             + [
-                pltpu.VMEM((tiles, 2 * rows, LANES), f32),
+                pltpu.VMEM((tiles, rows + 8, LANES), f32),
+                pltpu.VMEM((tiles, rows + 16, LANES), f32),
+                pltpu.VMEM((tiles, rows, LANES), f32),
                 pltpu.VMEM((span, LANES), f32),
                 pltpu.VMEM((span, 8, LANES), f32),
                 pltpu.VMEM((groups, span), f32),

time: 81.2 us -> 75.8 us (0.933)
  Pallas kernels: 73.2 us -> 67.8 us
    pallas_call x1, Pallas kernels: 73.2 us -> 67.8 us  [local_heads(): pl.pallas_call(functools.partial(kernel, n, tp), out_shape=[jax.ShapeDtyp...]
where the time goes in v3:
time: 75.8 us; the launch traced here: 75.5 us
  Pallas kernels  67.8 us (89%)
  local copies, waits for them, and re-layouts  7.01 us (9%)
    pallas_call x1, Pallas kernels, local_heads(): pl.pallas_call(functools.partial(kernel, n, tp), out_shape=[jax.ShapeDtyp...  67.8 us
    unnamed x19, local copies, waits for them, and re-layouts  7.01 us

profile of v3, /device:TPU:0, one launch (start us, length us, event | category | flops | bytes accessed | tf_op | source)
XLA Modules:
  0.0 75.5 jit_solution(3623835041273161515)
XLA Ops:
  0.6 67.8 %shard_map.162 = (bf16[128,1024]{1,0:T(8,128)(2,1)}, bf16[128,1024]{1,0:T(8,128)(2,1)}, bf16[128,1024]{1,0:T(8,128)(2,1)}, bf16[128,2048]{1,0:T(8,128)(2,1)}, bf...) custom-call(bf16[128,1024]{1,0:T(8,128)(2,1)} %q_in.1, bf16[128,1024]{1,0:T(8,128)(2,1)} %k_in.1, ...), custom_call_target="tpu_custom_call" | custom-call | tf_op jit(solution)/shard_map/pallas_call | solution.py:657
  68.5 0.0 copy-start.4
  68.5 0.0 copy-start.3
  68.5 1.7 %copy.25 = bf16[128,1024]{1,0:T(8,128)(2,1)} copy(bf16[128,1024]{1,0:T(8,128)(2,1)} %get-tuple-element.14) | data formatting | bytes 524288
  70.2 0.0 copy-done.4
  70.2 0.0 copy-start.2
  70.2 0.7 copy.26
  70.9 0.0 copy-done.3
  70.9 0.7 copy.27
  71.6 0.0 copy-done.2
  71.6 0.0 copy-start.1
  71.6 0.8 %copy.28 = bf16[128,2048]{1,0:T(8,128)(2,1)} copy(bf16[128,2048]{1,0:T(8,128)(2,1)S(1)} %copy-done.2) | data formatting | bytes 1048576
  72.4 0.4 copy-done.1
  72.9 0.0 copy-start
  72.9 0.8 %copy.29 = bf16[128,2048]{1,0:T(8,128)(2,1)} copy(bf16[128,2048]{1,0:T(8,128)(2,1)S(1)} %copy-done.1) | data formatting | bytes 1048576
  73.7 0.4 copy-done
  74.1 0.0 copy-start.5
  74.1 0.8 %copy.30 = bf16[128,2048]{1,0:T(8,128)(2,1)} copy(bf16[128,2048]{1,0:T(8,128)(2,1)S(1)} %copy-done) | data formatting | bytes 1048576
  74.9 0.0 copy-done.5
  74.9 0.6 copy.31
Async XLA Ops:
  68.5 1.7 %copy-start.4 = (bf16[128,1024]{1,0:T(8,128)(2,1)S(1)}, bf16[128,1024]{1,0:T(8,128)(2,1)}, u32[]{:S(2)}) copy-start(bf16[128,1024]{1,0:T(8,128)(2,1)} %get-tuple-element.15) | copy-start | bytes 786436
  68.5 2.4 %copy-start.3 = (bf16[128,1024]{1,0:T(8,128)(2,1)S(1)}, bf16[128,1024]{1,0:T(8,128)(2,1)}, u32[]{:S(2)}) copy-start(bf16[128,1024]{1,0:T(8,128)(2,1)} %get-tuple-element.16) | copy-start | bytes 786436
  70.2 1.4 %copy-start.2 = (bf16[128,2048]{1,0:T(8,128)(2,1)S(1)}, bf16[128,2048]{1,0:T(8,128)(2,1)}, u32[]{:S(2)}) copy-start(bf16[128,2048]{1,0:T(8,128)(2,1)} %get-tuple-element.17) | copy-start | bytes 1572868
  71.6 1.2 %copy-start.1 = (bf16[128,2048]{1,0:T(8,128)(2,1)S(1)}, bf16[128,2048]{1,0:T(8,128)(2,1)}, u32[]{:S(2)}) copy-start(bf16[128,2048]{1,0:T(8,128)(2,1)} %get-tuple-element.18) | copy-start | bytes 1572868
  72.9 1.2 %copy-start = (bf16[128,2048]{1,0:T(8,128)(2,1)S(1)}, bf16[128,2048]{1,0:T(8,128)(2,1)}, u32[]{:S(2)}) copy-start(bf16[128,2048]{1,0:T(8,128)(2,1)} %get-tuple-element.19) | copy-start | bytes 1572868
  74.1 0.8 %copy-start.5 = (f32[64,128]{1,0:T(8,128)S(1)}, f32[64,128]{1,0:T(8,128)}, u32[]{:S(2)}) copy-start(f32[64,128]{1,0:T(8,128)} %get-tuple-element.20) | copy-start | bytes 98308
